TPU v7x, 32 devices: a whole 2x2x4 slice. The times are simulated.
32 devices in a mesh: groups: 2 (over y), expert: 4 (over z), tensor: 2 (over x), inner: 2 (over core).
Axes of the slice: x: 2, y: 2, z: 4, core: 2. Of those that a mesh axis runs over, the one named last changes fastest.
Arguments:
- tokens: bfloat16 [1024, 7168], P(('groups', 'expert'), ('tensor', 'inner')), parts along dimension 0, may hold values from -6 to 6
- expert_ids: int32 [1024, 8], P(('groups', 'expert')), parts along dimension 0, may hold values from 0 to 31, all different within a row; in each aligned block of 128 rows (0 to 127, 128 to 255, ...) at most 96 rows name the same one
- gate_weights: float32 [1024, 8], P(('groups', 'expert')), parts along dimension 0, may hold values from 0.05 to 0.45
- base_weights: bfloat16 [3, 1024, 7168], P(None, 'expert', ('tensor', 'inner')), may hold values from -0.0625 to 0.0625
- in_factor: bfloat16 [3840, 7168], P('expert', ('tensor', 'inner')), may hold values from -0.0625 to 0.0625
- out_factors: bfloat16 [2, 3840, 1024], P(None, 'expert', ('tensor', 'inner')), may hold values from -0.375 to 0.375
- ranks: int32 [32], P('expert'), may hold values from 64 to 512, as said below
Outputs:
- mixed: bfloat16 [1024, 7168], P(('groups', 'expert'), ('tensor', 'inner')), parts along dimension 0
There are 2 independent parts, one for each index of `groups`. A program takes and returns all parts, laid end to end along the dimension named above; an argument that names none is the same for every part. Nothing has to cross between parts.
Inputs may be any that keep to these rules, and one draw needn't show every extreme that they name: `expert_ids`: in each aligned block of 128 tokens no expert is chosen more than 96 times, and some expert is chosen exactly 96 times; the experts of one token differ. The ranks of each aligned block of 8 experts sum to exactly 960.
All inputs are finite; a program needn't handle non-finite values.
Results may differ from a plain program's by a relative error of at most 0.023.
Values may be sent and summed in bfloat16 or wider, within the bound.
No kernel may reach another device: no remote copies, remote signals or barrier semaphores. Data moves between devices by JAX's collectives and lax.ppermute only.
A program may use at most 64 MiB of HBM per device.

v0:
```python
import jax
import jax.numpy as jnp
from jax import lax
from jax.sharding import PartitionSpec as P

RANK_MAX = 512


def on_device(tokens, expert_ids, gate_weights, base_weights, in_factor, out_factors, ranks):
    tok_rows, feat_slice = tokens.shape
    top_count = expert_ids.shape[1]
    owners = lax.axis_size("expert")
    local_count = ranks.shape[0]
    experts = local_count * owners
    capacity = min(tok_rows, 3 * tok_rows * top_count // experts)
    hidden_slice = out_factors.shape[2]
    width = RANK_MAX
    gathered = lax.all_gather(base_weights, "expert", axis=1, tiled=True)
    partial_value = jnp.einsum(
        "td,gfd->tgf", tokens, gathered[:2], preferred_element_type=jnp.float32
    )
    base_rows = lax.psum_scatter(
        partial_value.astype(jnp.bfloat16), ("tensor", "inner"), scatter_dimension=2, tiled=True
    )
    pairs = tok_rows * top_count
    flat_ids = expert_ids.reshape(pairs)
    columns = lax.broadcasted_iota(jnp.int32, (pairs, experts), 1)
    onehot = (flat_ids[:, None] == columns).astype(jnp.bfloat16)
    row_pos = lax.broadcasted_iota(jnp.int32, (pairs, pairs), 0)
    col_pos = lax.broadcasted_iota(jnp.int32, (pairs, pairs), 1)
    earlier = (row_pos > col_pos).astype(jnp.bfloat16)
    counts = jnp.dot(earlier, onehot, preferred_element_type=jnp.float32)
    slot = jnp.sum(counts * onehot.astype(jnp.float32), axis=1).astype(jnp.int32)
    owner_of = flat_ids // local_count
    member_of = flat_ids % local_count
    target = (member_of * owners + owner_of) * capacity + slot
    source_row = lax.broadcasted_iota(jnp.int32, (pairs,), 0) // top_count
    outgoing = jnp.zeros((local_count * owners * capacity, feat_slice), jnp.bfloat16)
    outgoing = outgoing.at[target].set(tokens[source_row])
    outgoing = outgoing.reshape(local_count, owners, capacity, feat_slice)
    arrived = lax.all_to_all(outgoing, "expert", split_axis=1, concat_axis=1, tiled=True)
    slots = owners * capacity
    arrived = arrived.reshape(local_count, slots, feat_slice)
    starts = jnp.cumsum(ranks) - ranks
    in_pad = jnp.concatenate([in_factor, jnp.zeros((width, feat_slice), jnp.bfloat16)], 0)
    out_pad = jnp.concatenate([out_factors, jnp.zeros((2, width, hidden_slice), jnp.bfloat16)], 1)
    within = lax.broadcasted_iota(jnp.int32, (1, width), 1)
    terms = []
    for member in range(local_count):
        window = lax.dynamic_slice_in_dim(in_pad, starts[member], width, 0)
        terms.append(
            lax.dot_general(
                arrived[member],
                window,
                (((1,), (1,)), ((), ())),
                preferred_element_type=jnp.float32,
            )
        )
    stacked = jnp.stack(
        [
            jnp.where(within < ranks[member], terms[member], jnp.float32(0.0))
            for member in range(local_count)
        ]
    )
    summed = lax.psum(stacked.astype(jnp.bfloat16), ("tensor", "inner"))
    latents = [summed[member] for member in range(local_count)]
    outputs = []
    for member in range(local_count):
        factor = lax.dynamic_slice_in_dim(out_pad, starts[member], width, 1)
        outputs.append(
            jnp.einsum(
                "rc,gcf->rgf", latents[member], factor, preferred_element_type=jnp.float32
            ).astype(jnp.bfloat16)
        )
    replies = jnp.stack(outputs).reshape(local_count, owners, capacity, 2, hidden_slice)
    returned = lax.all_to_all(replies, "expert", split_axis=1, concat_axis=1, tiled=True)
    returned = returned.reshape(local_count * owners * capacity, 2, hidden_slice)
    delta = returned[target].reshape(tok_rows, top_count, 2, hidden_slice)
    summed_rows = base_rows.astype(jnp.float32)[:, None] + delta.astype(jnp.float32)
    hidden = (jax.nn.silu(summed_rows[:, :, 0]) * summed_rows[:, :, 1]).astype(jnp.bfloat16)
    combined = jnp.sum(gate_weights[:, :, None] * hidden.astype(jnp.float32), axis=1).astype(
        jnp.bfloat16
    )
    full_hidden = lax.all_gather(combined, ("tensor", "inner"), axis=1, tiled=True)
    return jnp.dot(full_hidden, gathered[2], preferred_element_type=jnp.float32).astype(
        jnp.bfloat16
    )


def solution(mesh):
    return jax.shard_map(
        on_device,
        mesh=mesh,
        in_specs=(
            P(("groups", "expert"), ("tensor", "inner")),
            P(("groups", "expert"), None),
            P(("groups", "expert"), None),
            P(None, "expert", ("tensor", "inner")),
            P("expert", ("tensor", "inner")),
            P(None, "expert", ("tensor", "inner")),
            P("expert"),
        ),
        out_specs=P(("groups", "expert"), ("tensor", "inner")),
        check_vma=False,
    )
```

profile of v0, /device:TPU:0, one launch (start us, length us, event | category | flops | bytes accessed | tf_op | source)
XLA Modules:
  0.0 655.1 jit_solution(18073991329550731420)
XLA Ops:
  7.4 0.0 copy-start
  7.4 0.8 copy.40
  8.2 0.1 eq.12
  8.3 0.1 reshape.282
  8.4 0.5 fusion.52
  9.0 0.0 copy-done
  9.0 31.3 %scatter_custom_fusion = bf16[3072,1792]{1,0:T(8,128)(2,1)} fusion(s32[1024]{0:T(1024)S(1)} %bitcast.155, bf16[]{:T(256)} %constant.47.clone.1, bf16[128,1792]{1,0:T(8,128)(2,1)S(1)} %copy-done, s32[1024]{0:T(1024)S(1)} %broadcast_clamp_fusion.1), kind=kCustom, calls=%fused_computation.13 | custom fusion | bytes 11010050 | tf_op jit(solution)/shard_map/scatter | solution.py:39
  40.3 9.6 %copy.42 = bf16[8,4,96,1792]{3,2,0,1:T(8,128)(2,1)} copy(bf16[8,4,96,1792]{3,2,1,0:T(8,128)(2,1)} %bitcast.135) | data formatting | bytes 22020096 | tf_op jit(solution)/shard_map/reshape | solution.py:40
  50.0 6.5 all-to-all-start
  56.5 0.0 copy-done.3
  56.5 0.2 reduce-window.9
  56.6 0.7 fusion.94
  72.4 0.7 fusion.93
  73.1 0.6 iota_compare_fusion.15
  73.8 0.6 iota_compare_fusion.14
  74.4 0.6 iota_compare_fusion.13
  75.0 0.7 iota_compare_fusion.12
  75.7 0.6 iota_compare_fusion.11
  76.2 0.7 iota_compare_fusion.10
  76.9 0.6 iota_compare_fusion.9
  77.6 0.7 iota_compare_fusion.8
  78.2 218.9 %all-to-all-done = bf16[8,4,96,1792]{3,2,0,1:T(8,128)(2,1)} async-done(((bf16[8,4,96,1792]{3,2,0,1:T(8,128)(2,1)}), bf16[8,4,96,1792]{3,2,0,1:T(8,128)(2,1)}, u32[]{:S(2)}, u32[]{:S(2)}) %all-to-all-start) | async-done | bytes 11010080 | tf_op jit(solution)/shard_map/all_to_all | solution.py:41
  297.2 4.9 fusion.91
  302.1 0.3 copy-done.5
  302.4 1.9 fusion.50
  304.3 1.9 fusion.48
  306.2 1.9 fusion.46
  308.1 1.9 fusion.44
  310.0 1.9 fusion.42
  311.9 1.9 fusion.40
  313.8 1.9 fusion.38
  315.7 1.9 fusion.36
  317.6 0.0 all-reduce.4.cloned.1.call-update
  317.6 0.2 all-gather.2.cloned.1.call-start
  317.8 0.3 all-gather.2.cloned.1.call-update
  318.2 67.2 %all-reduce.4.cloned.1.call-done = bf16[8,384,512]{2,1,0:T(8,128)(2,1)} async-done(((bf16[8,384,512]{2,1,0:T(8,128)(2,1)}), bf16[8,384,512]{2,1,0:T(8,128)(2,1)}) %all-reduce.4.cloned.1.call-update) | async-done | bytes 3145744 | tf_op jit(solution)/shard_map/psum | solution.py:65
  385.4 1.6 convolution_convert_fusion.7
  387.1 1.5 convolution_convert_fusion.6
  388.7 0.5 convolution_convert_fusion.5
  389.2 0.5 convolution_convert_fusion.4
  389.8 0.5 convolution_convert_fusion.3
  390.3 0.5 convolution_convert_fusion.2
  390.9 0.5 convolution_convert_fusion.1
  391.4 0.5 convolution_convert_fusion
  392.0 1.9 copy.54
  393.9 4.7 all-to-all-start.1
  398.5 0.0 copy-start.4
  398.5 0.0 reduce-scatter.2.cloned.1.call-start
  398.6 179.9 %all-gather.2.cloned.1.call-done = bf16[3,1024,1792]{2,1,0:T(8,128)(2,1)} async-done(((bf16[3,256,1792]{2,1,0:T(8,128)(2,1)}), bf16[3,1024,1792]{2,1,0:T(8,128)(2,1)}) %all-gather.2.cloned.1.call-update) | async-done | bytes 11010064 | tf_op jit(solution)/shard_map/all_gather | solution.py:18
  578.4 6.3 fusion.16
  584.8 0.0 reduce-scatter.2.cloned.1.call-update
  584.8 0.0 copy-done.4
  584.8 0.1 copy.38
  584.9 19.8 %reduce-scatter.2.cloned.1.call-done = bf16[128,2,256]{2,0,1:T(8,128)(2,1)} async-done(((bf16[128,2,1024]{2,0,1:T(8,128)(2,1)}), bf16[128,2,256]{2,0,1:T(8,128)(2,1)}) %reduce-scatter.2.cloned.1.call-update) | async-done | bytes 131088 | tf_op jit(solution)/shard_map/reduce_scatter | solution.py:22
  604.7 1.0 copy.39
  605.8 0.0 all-to-all-done.1
  605.8 2.2 copy.51
  607.9 20.6 %copy.52 = bf16[3072,2,256]{2,1,0:T(2,128)(2,1)} copy(bf16[3072,2,256]{2,0,1:T(8,128)(2,1)S(1)} %bitcast.136) | data formatting | bytes 6291456 | tf_op jit(solution)/shard_map/reshape | solution.py:77
  628.5 6.1 gather_fusion
  634.6 1.3 convert_add_fusion
  635.9 1.6 fusion.92
  637.5 0.6 multiply_reduce_fusion
  638.1 5.8 all_gather.7
  643.8 3.5 fusion.7
  (20 shorter events, 0.3 us)
Async XLA Ops:
  7.4 1.7 copy-start
  50.0 6.5 copy-start.3
  50.0 247.2 %all-to-all-start = ((bf16[8,4,96,1792]{3,2,0,1:T(8,128)(2,1)}), bf16[8,4,96,1792]{3,2,0,1:T(8,128)(2,1)}, u32[]{:S(2)}, u32[]{:S(2)}) async-start(bf16[8,4,96,1792]{3,2,0,1:T(8,128)(2,1)} %copy.42), calls=%async_computation.1 | async-start | bytes 22020096 | tf_op jit(solution)/shard_map/all_to_all | solution.py:41
  56.5 329.0 %all-reduce.4.cloned.1.call-start = ((), (), s32[]{:S(2)}) async-start(), calls=%async_computation.5 | async-start | bytes 6291456 | tf_op jit(solution)/shard_map/psum | solution.py:65
  297.2 5.2 copy-start.5
  317.6 67.9 %copy-start.1 = (bf16[2,960,256]{2,1,0:T(8,128)(2,1)S(1)}, bf16[2,960,256]{2,1,0:T(8,128)(2,1)}, u32[]{:S(2)}) copy-start(bf16[2,960,256]{2,1,0:T(8,128)(2,1)} %param.12) | copy-start | bytes 2949124
  317.6 260.9 %all-gather.2.cloned.1.call-start = ((), (), s32[]{:S(2)}) async-start(), calls=%async_computation.3 | async-start | bytes 13762560 | tf_op jit(solution)/shard_map/all_gather | solution.py:18
  385.4 3.2 copy-start.2
  393.9 211.9 %all-to-all-start.1 = ((bf16[8,4,96,2,256]{4,2,0,3,1:T(8,128)(2,1)}), bf16[8,4,96,2,256]{4,2,0,3,1:T(8,128)(2,1)}, u32[]{:S(2)}, u32[]{:S(2)}) async-start(bf16[8,4,96,2,256]{4,2,0,3,1:T(8,128)(2,1)} %copy.54), calls=%async_computation.2 | async-start | bytes 6291456 | tf_op jit(solution)/shard_map/all_to_all | solution.py:76
  398.5 186.3 %copy-start.4 = (f32[128,8]{0,1:T(8,128)S(1)}, f32[128,8]{0,1:T(8,128)}, u32[]{:S(2)}) copy-start(f32[128,8]{0,1:T(8,128)} %param.9) | copy-start | bytes 12292
  398.5 206.2 %reduce-scatter.2.cloned.1.call-start = ((), (), s32[]{:S(2)}) async-start(), calls=%async_computation.4 | async-start | bytes 655360 | tf_op jit(solution)/shard_map/reduce_scatter | solution.py:22
Sparse Core Ops, SparseCore 0:
  317.7 67.6 all-reduce.3
  584.9 19.7 reduce-scatter.1
Sparse Core Ops, SparseCore 1:
  319.6 258.7 all-gather.1
where the time goes:
time: 664 us; the launch traced here: 655 us
  waiting for transfers between devices  486 us (73%)
  local copies, waits for them, and re-layouts  82.2 us (12%)
  matrix products  31.7 us (5%)
  between operations  30.7 us (5%)
  starting transfers between devices  11.4 us (2%)
  other arithmetic  7.15 us (1%)
    all_to_all x1, waiting for transfers between devices, on_device(): lax.all_to_all(outgoing, 'expert', split_axis=1, concat_axis=1, tiled=True)  219 us
    all_gather x1, waiting for transfers between devices, on_device(): gathered = lax.all_gather(base_weights, 'expert', axis=1, tiled=True)  180 us
    psum x1, waiting for transfers between devices, on_device(): summed = lax.psum(stacked.astype(jnp.bfloat16), ('tensor', 'inner'))  67.2 us
    scatter x1, local copies, waits for them, and re-layouts, on_device(): outgoing = outgoing.at[target].set(tokens[source_row])  31.3 us
    reshape x1, local copies, waits for them, and re-layouts, on_device(): returned.reshape(local_count * owners * capacity, 2, hidden_slice)  20.6 us
    reduce_scatter x1, waiting for transfers between devices, on_device(): lax.psum_scatter(partial_value.astype(jnp.bfloat16), ('tensor', 'inner'),...  19.8 us
    dot_general x8, matrix products, on_device(): lax.dot_general(arrived[member], window, (((1,), (1,)), ((), ())), prefer...  15.2 us
  transfers between devices with their start and end apart: 5, of which 4 were waited for; matrix products, arithmetic and copies ran while one was open for 3% of the time, Pallas kernels for 0%

commit v1 on v0

--- a/solution.py
+++ b/solution.py
@@ -62,7 +62,7 @@
             for member in range(local_count)
         ]
     )
-    summed = lax.psum(stacked.astype(jnp.bfloat16), ("tensor", "inner"))
+    summed = jnp.sum(lax.all_gather(stacked.astype(jnp.bfloat16), ("tensor", "inner")), axis=0)
     latents = [summed[member] for member in range(local_count)]
     outputs = []
     for member in range(local_count):

time: 664 us -> 738 us (1.11)
  waiting for transfers between devices: 486 us -> 558 us
  other arithmetic: 7.15 us -> 16.4 us
    all_gather x0 -> x1, waiting for transfers between devices: none -> 80.7 us  [on_device(): lax.all_gather(stacked.astype(jnp.bfloat16), ('tensor', 'inner'))]
    psum x1 -> x0, waiting for transfers between devices: 67.2 us -> none  [on_device(): summed = lax.psum(stacked.astype(jnp.bfloat16), ('tensor', 'inner'))]
    all_gather x1, waiting for transfers between devices: 180 us -> 238 us  [on_device(): gathered = lax.all_gather(base_weights, 'expert', axis=1, tiled=True)]
    reduce_sum x0 -> x1, other arithmetic: none -> 9.26 us  [on_device(): jnp.sum(lax.all_gather(stacked.astype(jnp.bfloat16), ('tensor', 'inner'))...]
  transfers between devices with their start and end apart: 5 -> 5, of which waited for: 4 -> 4; matrix products, arithmetic and copies ran while one was open for 3% -> 4% of each run, Pallas kernels for 0% -> 0%
where the time goes in v1:
time: 738 us; the launch traced here: 728 us
  waiting for transfers between devices  558 us (76%)
  local copies, waits for them, and re-layouts  75.4 us (10%)
  matrix products  32 us (4%)
  between operations  28.8 us (4%)
  other arithmetic  16.4 us (2%)
  starting transfers between devices  11.6 us (2%)
    all_gather x1, waiting for transfers between devices, on_device(): gathered = lax.all_gather(base_weights, 'expert', axis=1, tiled=True)  238 us
    all_to_all x1, waiting for transfers between devices, on_device(): lax.all_to_all(outgoing, 'expert', split_axis=1, concat_axis=1, tiled=True)  219 us
    all_gather x1, waiting for transfers between devices, on_device(): lax.all_gather(stacked.astype(jnp.bfloat16), ('tensor', 'inner'))  80.7 us
    scatter x1, local copies, waits for them, and re-layouts, on_device(): outgoing = outgoing.at[target].set(tokens[source_row])  24.4 us
    reshape x1, local copies, waits for them, and re-layouts, on_device(): returned.reshape(local_count * owners * capacity, 2, hidden_slice)  20.6 us
    reduce_scatter x1, waiting for transfers between devices, on_device(): lax.psum_scatter(partial_value.astype(jnp.bfloat16), ('tensor', 'inner'),...  19.8 us
    dot_general x8, matrix products, on_device(): lax.dot_general(arrived[member], window, (((1,), (1,)), ((), ())), prefer...  15.3 us
  transfers between devices with their start and end apart: 5, of which 4 were waited for; matrix products, arithmetic and copies ran while one was open for 4% of the time, Pallas kernels for 0%

profile of v1, /device:TPU:0, one launch (start us, length us, event | category | flops | bytes accessed | tf_op | source)
XLA Modules:
  0.0 728.4 jit_solution(5765432838375914047)
XLA Ops:
  6.5 0.0 copy-start
  6.5 0.8 copy.40
  7.4 0.1 eq.12
  7.5 0.1 reshape.405
  7.6 0.5 fusion.52
  8.2 24.4 %scatter_custom_fusion = bf16[3072,1792]{1,0:T(8,128)(2,1)} fusion(s32[1024]{0:T(1024)S(1)} %bitcast.155, bf16[]{:T(256)} %constant.48.clone.1, bf16[128,1792]{1,0:T(8,128)(2,1)S(1)} %copy-done, s32[1024]{0:T(1024)S(1)} %broadcast_clamp_fusion.1), kind=kCustom, calls=%fused_computation.13 | custom fusion | bytes 11010050 | tf_op jit(solution)/shard_map/scatter | solution.py:39
  32.6 9.6 %copy.42 = bf16[8,4,96,1792]{3,2,0,1:T(8,128)(2,1)} copy(bf16[8,4,96,1792]{3,2,1,0:T(8,128)(2,1)} %bitcast.135) | data formatting | bytes 22020096 | tf_op jit(solution)/shard_map/reshape | solution.py:40
  42.2 6.5 all-to-all-start
  48.7 0.2 reduce-window.9
  48.9 0.7 fusion.94
  64.7 0.7 fusion.93
  65.4 0.6 iota_compare_fusion.15
  66.0 0.6 iota_compare_fusion.14
  66.7 0.6 iota_compare_fusion.13
  67.3 0.7 iota_compare_fusion.12
  67.9 0.6 iota_compare_fusion.11
  68.5 0.7 iota_compare_fusion.10
  69.2 0.6 iota_compare_fusion.9
  69.9 0.7 iota_compare_fusion.8
  70.5 218.9 %all-to-all-done = bf16[8,4,96,1792]{3,2,0,1:T(8,128)(2,1)} async-done(((bf16[8,4,96,1792]{3,2,0,1:T(8,128)(2,1)}), bf16[8,4,96,1792]{3,2,0,1:T(8,128)(2,1)}, u32[]{:S(2)}, u32[]{:S(2)}) %all-to-all-start) | async-done | bytes 11010080 | tf_op jit(solution)/shard_map/all_to_all | solution.py:41
  289.4 4.9 fusion.91
  294.4 0.3 copy-done.5
  294.6 1.9 fusion.50
  296.5 1.9 fusion.48
  298.4 1.9 fusion.46
  300.3 1.9 fusion.44
  302.3 1.9 fusion.42
  304.2 1.9 fusion.40
  306.1 1.9 fusion.38
  308.0 1.9 fusion.36
  309.9 0.0 all-gather.5.cloned.1.call-update
  309.9 0.2 all-gather.3.cloned.1.call-start
  310.2 0.5 all-gather.3.cloned.1.call-update
  310.7 0.0 copy-start.1
  310.7 80.7 %all-gather.5.cloned.1.call-done = bf16[4,8,384,512]{3,2,1,0:T(8,128)(2,1)} async-done(((bf16[1,8,384,512]{3,2,1,0:T(8,128)(2,1)}), bf16[4,8,384,512]{3,2,1,0:T(8,128)(2,1)}) %all-gather.5.cloned.1.call-update) | async-done | bytes 12582928 | tf_op jit(solution)/shard_map/all_gather | solution.py:65
  391.4 9.3 %reduce_sum.31 = bf16[8,384,512]{2,1,0:T(8,128)(2,1)} reduce(bf16[4,8,384,512]{3,2,1,0:T(8,128)(2,1)} %all-gather.5.cloned.1.call-done, bf16[]{:T(256)} %constant.48.clone.1), dimensions={0}, to_apply=%region_4.5 | reduce | flops 4718592 | bytes 15728642 | tf_op jit(solution)/shard_map/reduce_sum | solution.py:65
  400.7 1.7 convolution_convert_fusion.7
  402.4 1.6 convolution_convert_fusion.6
  404.1 0.5 convolution_convert_fusion.5
  404.6 0.5 convolution_convert_fusion.4
  405.2 0.5 convolution_convert_fusion.3
  405.7 0.5 convolution_convert_fusion.2
  406.3 0.5 convolution_convert_fusion.1
  406.8 0.5 convolution_convert_fusion
  407.4 2.0 copy.54
  409.3 4.6 all-to-all-start.1
  414.0 0.0 copy-start.4
  414.0 0.3 reduce-scatter.2.cloned.1.call-start
  414.3 238.4 %all-gather.3.cloned.1.call-done = bf16[3,1024,1792]{2,1,0:T(8,128)(2,1)} async-done(((bf16[3,256,1792]{2,1,0:T(8,128)(2,1)}), bf16[3,1024,1792]{2,1,0:T(8,128)(2,1)}) %all-gather.3.cloned.1.call-update) | async-done | bytes 11010064 | tf_op jit(solution)/shard_map/all_gather | solution.py:18
  652.7 6.4 fusion.16
  659.1 0.0 reduce-scatter.2.cloned.1.call-update
  659.1 0.0 copy-done.4
  659.1 0.1 copy.38
  659.2 19.8 %reduce-scatter.2.cloned.1.call-done = bf16[128,2,256]{2,0,1:T(8,128)(2,1)} async-done(((bf16[128,2,1024]{2,0,1:T(8,128)(2,1)}), bf16[128,2,256]{2,0,1:T(8,128)(2,1)}) %reduce-scatter.2.cloned.1.call-update) | async-done | bytes 131088 | tf_op jit(solution)/shard_map/reduce_scatter | solution.py:22
  679.0 1.0 copy.39
  680.0 0.0 all-to-all-done.1
  680.1 2.2 copy.51
  682.2 20.6 %copy.52 = bf16[3072,2,256]{2,1,0:T(2,128)(2,1)} copy(bf16[3072,2,256]{2,0,1:T(8,128)(2,1)S(1)} %bitcast.136) | data formatting | bytes 6291456 | tf_op jit(solution)/shard_map/reshape | solution.py:77
  702.8 6.1 gather_fusion
  708.9 1.3 convert_add_fusion
  710.2 1.6 fusion.92
  711.8 0.6 multiply_reduce_fusion
  712.4 5.8 all_gather.12
  718.1 3.5 fusion.7
  (21 shorter events, 0.3 us)
Async XLA Ops:
  6.5 1.7 copy-start
  42.2 6.5 copy-start.3
  42.2 247.2 %all-to-all-start = ((bf16[8,4,96,1792]{3,2,0,1:T(8,128)(2,1)}), bf16[8,4,96,1792]{3,2,0,1:T(8,128)(2,1)}, u32[]{:S(2)}, u32[]{:S(2)}) async-start(bf16[8,4,96,1792]{3,2,0,1:T(8,128)(2,1)} %copy.42), calls=%async_computation.1 | async-start | bytes 22020096 | tf_op jit(solution)/shard_map/all_to_all | solution.py:41
  48.7 342.7 %all-gather.5.cloned.1.call-start = ((), (), s32[]{:S(2)}) async-start(), calls=%async_computation.5 | async-start | bytes 15728640 | tf_op jit(solution)/shard_map/all_gather | solution.py:65
  289.4 5.2 copy-start.5
  309.9 342.7 %all-gather.3.cloned.1.call-start = ((), (), s32[]{:S(2)}) async-start(), calls=%async_computation.3 | async-start | bytes 13762560 | tf_op jit(solution)/shard_map/all_gather | solution.py:18
  310.7 90.0 %copy-start.1 = (bf16[2,960,256]{2,1,0:T(8,128)(2,1)S(1)}, bf16[2,960,256]{2,1,0:T(8,128)(2,1)}, u32[]{:S(2)}) copy-start(bf16[2,960,256]{2,1,0:T(8,128)(2,1)} %param.12) | copy-start | bytes 2949124
  400.7 3.4 copy-start.2
  409.3 270.7 %all-to-all-start.1 = ((bf16[8,4,96,2,256]{4,2,0,3,1:T(8,128)(2,1)}), bf16[8,4,96,2,256]{4,2,0,3,1:T(8,128)(2,1)}, u32[]{:S(2)}, u32[]{:S(2)}) async-start(bf16[8,4,96,2,256]{4,2,0,3,1:T(8,128)(2,1)} %copy.54), calls=%async_computation.2 | async-start | bytes 6291456 | tf_op jit(solution)/shard_map/all_to_all | solution.py:76
  414.0 245.1 %copy-start.4 = (f32[128,8]{0,1:T(8,128)S(1)}, f32[128,8]{0,1:T(8,128)}, u32[]{:S(2)}) copy-start(f32[128,8]{0,1:T(8,128)} %param.9) | copy-start | bytes 12292
  414.0 265.0 %reduce-scatter.2.cloned.1.call-start = ((), (), s32[]{:S(2)}) async-start(), calls=%async_computation.4 | async-start | bytes 655360 | tf_op jit(solution)/shard_map/reduce_scatter | solution.py:22
Sparse Core Ops, SparseCore 0:
  310.1 81.3 all-gather.4
  393.0 259.6 all-gather.2
  659.2 19.7 reduce-scatter.1
